TPU v7x, 128 devices: a whole 4x4x4 slice. The times are simulated.
128 devices in a mesh: row: 8 (over z, core), col: 16 (over y, x).
Axes of the slice: x: 4, y: 4, z: 4, core: 2. Of those that a mesh axis runs over, the one named last changes fastest.
Arguments:
- emb: bfloat16 [524288, 512], P(('row', 'col')), may hold values from -6 to 6
- tiles: bfloat16 [2048, 4, 256, 256], P(('row', 'col')), may hold values from -0.375 to 0.375
- msg_src: int32 [2048, 4], P(('row', 'col')), may hold values from 0 to 15
- msg_dst: int32 [2048, 4], P(('row', 'col')), may hold values from 0 to 16, as said below
- msg_count: int32 [2048, 4], P(('row', 'col')), may hold values from 1 to 256
- weight: bfloat16 [512, 512], replicated, may hold values from -0.25 to 0.25
- docs: bfloat16 [512, 512], P('row'), may hold values from -0.059814453 to 0.099609375
- doc_labels: int32 [512, 8], replicated, may hold values from 0 to 524287
Outputs:
- hidden: bfloat16 [524288, 512], P(('row', 'col'))
- grad_docs: float32 [512, 512], P('row')
- grad_weight: float32 [512, 512], replicated
Inputs may be any that keep to these rules, and one draw needn't show every extreme that they name: For each sending device and each column of its row, the used slots (msg_dst below 16) come first and 16 marks an unused slot. In every row of devices some column receives all 4 slots used from every sender of that row.
All inputs are finite; a program needn't handle non-finite values.
Results may differ from a plain program's by a relative error of at most 0.0052.
Values may be sent and summed in bfloat16 or wider, within the bound.
No kernel may reach another device: no remote copies, remote signals or barrier semaphores. Data moves between devices by JAX's collectives and lax.ppermute only.
A program may use at most 192 MiB of HBM per device.

v0:
```python
import jax
import jax.numpy as jnp
from jax import lax
from jax.sharding import PartitionSpec as P


def per_device(emb, tiles, msg_src, msg_dst, msg_count, weight, docs, doc_labels):
    n_col = lax.axis_size("col")
    n_row = lax.axis_size("row")
    label_dev, width = emb.shape
    blk = tiles.shape[-1]
    cap = tiles.shape[1]
    blk_dev = label_dev // blk
    labels_total = float(label_dev * n_row * n_col)
    pos_count = doc_labels.shape[1]
    own_blocks = emb.reshape(blk_dev, blk, width)
    picked = own_blocks[msg_src]
    messages = jnp.einsum(
        "pqij,pqjd->pqid", tiles, picked, preferred_element_type=jnp.float32
    ).astype(jnp.bfloat16)
    received, dst_seen, cnt_seen = (
        lax.all_to_all(messages, "col", split_axis=0, concat_axis=0, tiled=True),
        lax.all_to_all(
            msg_dst.astype(jnp.bfloat16), "col", split_axis=0, concat_axis=0, tiled=True
        ),
        lax.all_to_all(
            msg_count.astype(jnp.bfloat16), "col", split_axis=0, concat_axis=0, tiled=True
        ),
    )
    slots_all = n_col * cap
    block_ids = jnp.arange(blk_dev, dtype=jnp.float32)
    hot = (dst_seen.astype(jnp.float32).reshape(1, slots_all) == block_ids[:, None]).astype(
        jnp.float32
    )
    weighted = hot * cnt_seen.astype(jnp.float32).reshape(1, slots_all)
    total = jnp.dot(
        weighted.astype(jnp.bfloat16),
        received.reshape(slots_all, blk * width),
        preferred_element_type=jnp.float32,
    ).reshape(blk_dev, blk, width)
    total = total + float(blk) * own_blocks.astype(jnp.float32)
    denom = float(blk) + jnp.sum(weighted, axis=1)
    agg = (total / denom[:, None, None]).astype(jnp.bfloat16).reshape(label_dev, width)
    pre = jnp.dot(agg, weight, preferred_element_type=jnp.float32)
    hidden = jax.nn.silu(pre).astype(jnp.bfloat16)
    device = lax.axis_index("row") * n_col + lax.axis_index("col")
    label_ids = device * label_dev + jnp.arange(label_dev, dtype=jnp.int32)
    piece = lax.all_gather(docs, "row", axis=0, tiled=True)
    scores = jnp.einsum("nd,ld->nl", piece, hidden, preferred_element_type=jnp.float32)
    positive = doc_labels[:, 0:1] == label_ids[None, :]
    for which in range(1, pos_count):
        positive = positive | (doc_labels[:, which : which + 1] == label_ids[None, :])
    prob = jax.nn.sigmoid(scores)
    dscore = jnp.where(positive, (prob - 1.0) / float(pos_count), prob / labels_total).astype(
        jnp.bfloat16
    )
    rows_grad = jnp.dot(dscore, hidden, preferred_element_type=jnp.float32)
    dhid = jnp.einsum("nl,nd->ld", dscore, piece, preferred_element_type=jnp.float32)
    doc_grad = rows_grad
    dhid, doc_grad = (dhid, doc_grad)
    sig = jax.nn.sigmoid(pre)
    dpre = (dhid * sig * (1.0 + pre * (1.0 - sig))).astype(jnp.bfloat16)
    weight_part = jnp.einsum("la,lb->ab", agg, dpre, preferred_element_type=jnp.float32)
    grad_weight = lax.psum(weight_part, ("row", "col"))
    row_share = lax.psum_scatter(doc_grad, "row", scatter_dimension=0, tiled=True)
    grad_docs = lax.psum(row_share, "col")
    return (hidden, grad_docs, grad_weight)


def solution(mesh):
    in_specs = (
        P(("row", "col"), None),
        P(("row", "col"), None, None, None),
        P(("row", "col"), None),
        P(("row", "col"), None),
        P(("row", "col"), None),
        P(),
        P("row", None),
        P(),
    )
    out_specs = (P(("row", "col"), None), P("row", None), P())
    return jax.shard_map(
        per_device, mesh=mesh, in_specs=in_specs, out_specs=out_specs, check_vma=False
    )
```

profile of v0, /device:TPU:0, one launch (start us, length us, event | category | flops | bytes accessed | tf_op | source)
XLA Modules:
  0.0 621.5 jit_solution(9641399624754386184)
XLA Ops:
  8.0 0.7 convert_bitcast_fusion.2
  8.8 0.7 copy.23
  9.5 7.1 %all-to-all-start = ((bf16[16,1,4]{2,1,0:T(2,128)(2,1)}), bf16[16,1,4]{2,1,0:T(2,128)(2,1)S(1)}, u32[]{:S(2)}, u32[]{:S(2)}) async-start(bf16[16,1,4]{2,1,0:T(2,128)(2,1)} %copy.23), calls=%async_computation | async-start | bytes 16384 | tf_op jit(solution)/shard_map/all_to_all | solution.py:23
  16.6 0.7 convert_bitcast_fusion.1
  17.3 0.7 copy.24
  18.9 9.8 %gather_fusion = bf16[64,256,512]{2,1,0:T(8,128)(2,1)} fusion(bf16[16,256,512]{2,1,0:T(8,128)(2,1)} %bitcast.53, s32[1024]{0:T(1024)S(1)} %pad_clamp_fusion), kind=kCustom, calls=%fused_computation | custom fusion | bytes 33554688 | tf_op jit(solution)/shard_map/gather | solution.py:17
  28.6 7.2 %all-to-all-start.1 = ((bf16[16,1,4]{2,1,0:T(2,128)(2,1)}), bf16[16,1,4]{2,1,0:T(2,128)(2,1)S(1)}, u32[]{:S(2)}, u32[]{:S(2)}) async-start(bf16[16,1,4]{2,1,0:T(2,128)(2,1)} %copy.24), calls=%async_computation.1 | async-start | bytes 16384 | tf_op jit(solution)/shard_map/all_to_all | solution.py:26
  35.9 19.3 %convert_bitcast_fusion = bf16[16,4,256,512]{2,3,1,0:T(8,128)(2,1)} fusion(bf16[16,4,256,512]{3,2,1,0:T(8,128)(2,1)} %bitcast.52, bf16[16,4,256,256]{3,2,1,0:T(8,128)(2,1)} %param.9), kind=kOutput, calls=%fused_computation.4 | convolution fusion | flops 4303355904 | bytes 41943040 | tf_op jit(solution)/shard_map/pqij,pqjd->pqid/dot_general | solution.py:18
  55.1 7.4 %all-to-all-start.2 = ((bf16[16,4,256,512]{2,3,1,0:T(8,128)(2,1)}), bf16[16,4,256,512]{2,3,1,0:T(8,128)(2,1)}, u32[]{:S(2)}, u32[]{:S(2)}) async-start(bf16[16,4,256,512]{2,3,1,0:T(8,128)(2,1)} %convert_bitcast_fusion), calls=%async_computation.2 | async-start | bytes 33554432 | tf_op jit(solution)/shard_map/all_to_all | solution.py:22
  62.7 14.5 %all_gather.3 = bf16[512,512]{1,0:T(8,128)(2,1)S(1)} all-gather(bf16[64,512]{1,0:T(8,128)(2,1)S(1)} %copy-done.5), channel_id=1, replica_groups=mesh['row'=8,'col'=16] {'row'}, dimensions={0}, use_global_device_ids=true | all-gather | bytes 589824 | tf_op jit(solution)/shard_map/all_gather | solution.py:48
  77.5 229.1 %all-to-all-done.2 = bf16[16,4,256,512]{2,3,1,0:T(8,128)(2,1)} async-done(((bf16[16,4,256,512]{2,3,1,0:T(8,128)(2,1)}), bf16[16,4,256,512]{2,3,1,0:T(8,128)(2,1)}, u32[]{:S(2)}, u32[]{:S(2)}) %all-to-all-start.2) | async-done | bytes 16777248 | tf_op jit(solution)/shard_map/all_to_all | solution.py:22
  306.7 24.3 %copy.33 = bf16[8,8,256,512]{3,1,2,0:T(8,128)(2,1)} copy(bf16[8,8,256,512]{2,3,1,0:T(8,128)(2,1)} %bitcast.36) | data formatting | bytes 33554432
  331.0 9.2 %divide_convert_fusion = bf16[16,256,512]{2,0,1:T(8,128)(2,1)S(1)} fusion(bf16[16,256,512]{2,1,0:T(8,128)(2,1)} %bitcast.54, f32[16]{0:T(128)S(1)} %broadcast_add_fusion, f32[64]{0:T(128)S(1)} %reshape.48, f32[64]{0:T(128)S(1)} %reshape.47, bf16[8,8,256,512]{3,1,2,0:T(8,128)(2,1)} %copy.33), kind=kOutput, calls=%fused_computation.10 | convolution fusion | flops 278923264 | bytes 25166400 | tf_op jit(solution)/shard_map/dot_general | solution.py:36
  340.2 2.4 copy.30
  342.6 5.7 multiply_convert_fusion.1
  348.3 10.1 %fusion.3 = bf16[512,4096]{0,1:T(8,128)(2,1)S(1)} fusion(bf16[4096,512]{1,0:T(8,128)(2,1)S(1)} %get-tuple-element.13, bf16[512,512]{1,0:T(8,128)(2,1)S(1)} %all_gather.3, s32[512]{0:T(512)S(1)} %bitcast.63, s32[512]{0:T(512)S(1)} %bitcast.64, s32[512]{0:T(512)S(1)} %bitcast.58, s32[512]{0:T(512)S(1)} %bitcast.59, s32[512]{0:T(512)S(1)} %bitcast.60, ...), kind=kOutput, calls=%fused_computation.6 | convolution fusion | flops 2195718144 | bytes 8945664 | tf_op jit(solution)/shard_map/nd,ld->nl/dot_general | solution.py:49
  358.4 1.9 copy-done.3
  360.3 3.3 fusion.15
  363.9 12.6 %fusion.6 = f32[512,512]{1,0:T(8,128)} fusion(bf16[4096,512]{1,0:T(8,128)(2,1)} %bitcast.56, f32[4096,512]{1,0:T(8,128)} %get-tuple-element.12, bf16[512,4096]{0,1:T(8,128)(2,1)} %copy-done.3, bf16[512,512]{1,0:T(8,128)(2,1)S(1)} %all_gather.3), kind=kOutput, calls=%fused_computation.11 | convolution fusion | flops 4313841664 | bytes 18350080 | tf_op jit(solution)/shard_map/la,lb->ab/dot_general | solution.py:63
  376.6 21.8 %reduce-scatter.2.cloned.1.call-done = f32[64,512]{1,0:T(8,128)} async-done(((f32[512,512]{1,0:T(8,128)}), f32[64,512]{1,0:T(8,128)}) %reduce-scatter.2.cloned.1.call-update) | async-done | bytes 131088 | tf_op jit(solution)/shard_map/reduce_scatter | solution.py:65
  398.5 127.3 %all-reduce.5.cloned.1.call-done = f32[512,512]{1,0:T(8,128)} async-done(((f32[512,512]{1,0:T(8,128)}), f32[512,512]{1,0:T(8,128)}) %all-reduce.5.cloned.1.call-update) | async-done | bytes 1048592 | tf_op jit(solution)/shard_map/psum | solution.py:64
  525.7 84.6 %all-reduce.3.cloned.1.call-done = f32[64,512]{1,0:T(8,128)} async-done(((f32[64,512]{1,0:T(8,128)}), f32[64,512]{1,0:T(8,128)}) %all-reduce.3.cloned.1.call-update) | async-done | bytes 131088 | tf_op jit(solution)/shard_map/psum | solution.py:66
  610.3 1.6 copy.44
  611.8 2.3 copy.45
  (33 shorter events, 1.7 us)
Async XLA Ops:
  8.0 334.6 %copy-start = (bf16[512,512]{1,0:T(8,128)(2,1)S(1)}, bf16[512,512]{1,0:T(8,128)(2,1)}, u32[]{:S(2)}) copy-start(bf16[512,512]{1,0:T(8,128)(2,1)} %param.13) | copy-start | bytes 1572868
  9.5 19.2 %all-to-all-start = ((bf16[16,1,4]{2,1,0:T(2,128)(2,1)}), bf16[16,1,4]{2,1,0:T(2,128)(2,1)S(1)}, u32[]{:S(2)}, u32[]{:S(2)}) async-start(bf16[16,1,4]{2,1,0:T(2,128)(2,1)} %copy.23), calls=%async_computation | async-start | bytes 16384 | tf_op jit(solution)/shard_map/all_to_all | solution.py:23
  28.6 26.5 %all-to-all-start.1 = ((bf16[16,1,4]{2,1,0:T(2,128)(2,1)}), bf16[16,1,4]{2,1,0:T(2,128)(2,1)S(1)}, u32[]{:S(2)}, u32[]{:S(2)}) async-start(bf16[16,1,4]{2,1,0:T(2,128)(2,1)} %copy.24), calls=%async_computation.1 | async-start | bytes 16384 | tf_op jit(solution)/shard_map/all_to_all | solution.py:26
  55.1 7.5 %copy-start.6 = (s32[512,8]{0,1:T(8,128)S(1)}, s32[512,8]{0,1:T(8,128)}, u32[]{:S(2)}) copy-start(s32[512,8]{0,1:T(8,128)} %param.15) | copy-start | bytes 49156
  55.1 7.5 %copy-start.5 = (bf16[64,512]{1,0:T(8,128)(2,1)S(1)}, bf16[64,512]{1,0:T(8,128)(2,1)}, u32[]{:S(2)}) copy-start(bf16[64,512]{1,0:T(8,128)(2,1)} %param.14) | copy-start | bytes 196612
  55.1 251.5 %all-to-all-start.2 = ((bf16[16,4,256,512]{2,3,1,0:T(8,128)(2,1)}), bf16[16,4,256,512]{2,3,1,0:T(8,128)(2,1)}, u32[]{:S(2)}, u32[]{:S(2)}) async-start(bf16[16,4,256,512]{2,3,1,0:T(8,128)(2,1)} %convert_bitcast_fusion), calls=%async_computation.2 | async-start | bytes 33554432 | tf_op jit(solution)/shard_map/all_to_all | solution.py:22
  62.6 335.9 %reduce-scatter.2.cloned.1.call-start = ((), (), s32[]{:S(2)}) async-start(), calls=%async_computation.4 | async-start | bytes 1179648 | tf_op jit(solution)/shard_map/reduce_scatter | solution.py:65
  342.6 5.7 copy-start.4
  348.3 10.1 %copy-start.2 = (bf16[4096,512]{1,0:T(8,128)(2,1)}, bf16[4096,512]{1,0:T(8,128)(2,1)S(1)}, u32[]{:S(2)}) copy-start(bf16[4096,512]{1,0:T(8,128)(2,1)S(1)} %get-tuple-element.13) | copy-start | bytes 12582916
  358.3 1.9 copy-start.3
  363.6 162.1 %all-reduce.5.cloned.1.call-start = ((), (), s32[]{:S(2)}) async-start(), calls=%async_computation.6 | async-start | bytes 2097152 | tf_op jit(solution)/shard_map/psum | solution.py:64
  363.9 250.2 %copy-start.1 = (bf16[512,512]{1,0:T(8,128)(2,1)S(1)}, bf16[512,512]{1,0:T(8,128)(2,1)}, u32[]{:S(2)}) copy-start(bf16[512,512]{1,0:T(8,128)(2,1)} %param.13) | copy-start | bytes 1572868
  376.6 233.7 %all-reduce.3.cloned.1.call-start = ((), (), s32[]{:S(2)}) async-start(), calls=%async_computation.5 | async-start | bytes 262144 | tf_op jit(solution)/shard_map/psum | solution.py:66
Sparse Core Ops, SparseCore 0:
  363.8 34.6 reduce-scatter.1
Sparse Core Ops, SparseCore 1:
  376.6 149.0 all-reduce.4
  528.8 81.4 all-reduce.2
where the time goes:
time: 623 us; the launch traced here: 622 us
  waiting for transfers between devices  463 us (74%)
  matrix products  60.1 us (10%)
  local copies, waits for them, and re-layouts  44 us (7%)
  starting transfers between devices  22.1 us (4%)
  between operations  15.7 us (3%)
  blocking collectives  14.5 us (2%)
    all_to_all x1, waiting for transfers between devices, per_device(): lax.all_to_all(messages, 'col', split_axis=0, concat_axis=0, tiled=True)  229 us
    psum x1, waiting for transfers between devices, per_device(): grad_weight = lax.psum(weight_part, ('row', 'col'))  127 us
    psum x1, waiting for transfers between devices, per_device(): grad_docs = lax.psum(row_share, 'col')  84.6 us
    unnamed x17, local copies, waits for them, and re-layouts  30.1 us
    reduce_scatter x1, waiting for transfers between devices, per_device(): lax.psum_scatter(doc_grad, 'row', scatter_dimension=0, tiled=True)  21.8 us
    dot_general x1, matrix products, per_device(): jnp.einsum('pqij,pqjd->pqid', tiles, picked, preferred_element_type=jnp.f...  19.3 us
    all_gather x1, blocking collectives, per_device(): piece = lax.all_gather(docs, 'row', axis=0, tiled=True)  14.5 us
    dot_general x1, matrix products, per_device(): jnp.einsum('la,lb->ab', agg, dpre, preferred_element_type=jnp.float32)  12.6 us
  transfers between devices with their start and end apart: 6, of which 4 were waited for; matrix products, arithmetic and copies ran while one was open for 7% of the time, Pallas kernels for 0%

commit v1 on v0

--- a/solution.py
+++ b/solution.py
@@ -63,7 +63,11 @@
     weight_part = jnp.einsum("la,lb->ab", agg, dpre, preferred_element_type=jnp.float32)
     grad_weight = lax.psum(weight_part, ("row", "col"))
     row_share = lax.psum_scatter(doc_grad, "row", scatter_dimension=0, tiled=True)
-    grad_docs = lax.psum(row_share, "col")
+    grad_docs = row_share
+    for hop in (1, 2, 4, 8):
+        grad_docs = grad_docs + lax.ppermute(
+            grad_docs, "col", [(dev, dev ^ hop) for dev in range(16)]
+        )
     return (hidden, grad_docs, grad_weight)
 
 

time: 623 us -> 571 us (0.917)
  waiting for transfers between devices: 463 us -> 402 us
  starting transfers between devices: 22.1 us -> 30.8 us
    psum x1 -> x0, waiting for transfers between devices: 84.6 us -> none  [per_device(): grad_docs = lax.psum(row_share, 'col')]
    reduce_scatter x1, waiting for transfers between devices: 21.8 us -> 34.4 us  [per_device(): lax.psum_scatter(doc_grad, 'row', scatter_dimension=0, tiled=True)]
    ppermute x0 -> x4, waiting for transfers between devices: none -> 11.7 us  [per_device(): lax.ppermute(grad_docs, 'col', [(dev, dev ^ hop) for dev in range(16)])]
    ppermute x0 -> x4, starting transfers between devices: none -> 8.93 us  [per_device(): lax.ppermute(grad_docs, 'col', [(dev, dev ^ hop) for dev in range(16)])]
    unnamed x17 -> x18, local copies, waits for them, and re-layouts: 30.1 us -> 28.5 us
  transfers between devices with their start and end apart: 6 -> 9, of which waited for: 4 -> 6; matrix products, arithmetic and copies ran while one was open for 7% -> 8% of each run, Pallas kernels for 0% -> 0%
where the time goes in v1:
time: 571 us; the launch traced here: 568 us
  waiting for transfers between devices  402 us (70%)
  matrix products  60.1 us (11%)
  local copies, waits for them, and re-layouts  42.4 us (7%)
  starting transfers between devices  30.8 us (5%)
  between operations  15.7 us (3%)
  blocking collectives  14.5 us (3%)
    all_to_all x1, waiting for transfers between devices, per_device(): lax.all_to_all(messages, 'col', split_axis=0, concat_axis=0, tiled=True)  229 us
    psum x1, waiting for transfers between devices, per_device(): grad_weight = lax.psum(weight_part, ('row', 'col'))  127 us
    reduce_scatter x1, waiting for transfers between devices, per_device(): lax.psum_scatter(doc_grad, 'row', scatter_dimension=0, tiled=True)  34.4 us
    unnamed x18, local copies, waits for them, and re-layouts  28.5 us
    dot_general x1, matrix products, per_device(): jnp.einsum('pqij,pqjd->pqid', tiles, picked, preferred_element_type=jnp.f...  19.2 us
    all_gather x1, blocking collectives, per_device(): piece = lax.all_gather(docs, 'row', axis=0, tiled=True)  14.5 us
    dot_general x1, matrix products, per_device(): jnp.einsum('la,lb->ab', agg, dpre, preferred_element_type=jnp.float32)  12.6 us
    ppermute x4, waiting for transfers between devices, per_device(): lax.ppermute(grad_docs, 'col', [(dev, dev ^ hop) for dev in range(16)])  11.7 us
  transfers between devices with their start and end apart: 9, of which 6 were waited for; matrix products, arithmetic and copies ran while one was open for 8% of the time, Pallas kernels for 0%

profile of v1, /device:TPU:0, one launch (start us, length us, event | category | flops | bytes accessed | tf_op | source)
XLA Modules:
  0.0 568.5 jit_solution(17761258584590048342)
XLA Ops:
  9.5 7.1 %all-to-all-start = ((bf16[16,1,4]{2,1,0:T(2,128)(2,1)}), bf16[16,1,4]{2,1,0:T(2,128)(2,1)S(1)}, u32[]{:S(2)}, u32[]{:S(2)}) async-start(bf16[16,1,4]{2,1,0:T(2,128)(2,1)} %copy.23), calls=%async_computation | async-start | bytes 16384 | tf_op jit(solution)/shard_map/all_to_all | solution.py:23
  18.9 9.8 %gather_fusion = bf16[64,256,512]{2,1,0:T(8,128)(2,1)} fusion(bf16[16,256,512]{2,1,0:T(8,128)(2,1)} %bitcast.53, s32[1024]{0:T(1024)S(1)} %pad_clamp_fusion), kind=kCustom, calls=%fused_computation | custom fusion | bytes 33554688 | tf_op jit(solution)/shard_map/gather | solution.py:17
  28.7 7.2 %all-to-all-start.1 = ((bf16[16,1,4]{2,1,0:T(2,128)(2,1)}), bf16[16,1,4]{2,1,0:T(2,128)(2,1)S(1)}, u32[]{:S(2)}, u32[]{:S(2)}) async-start(bf16[16,1,4]{2,1,0:T(2,128)(2,1)} %copy.24), calls=%async_computation.1 | async-start | bytes 16384 | tf_op jit(solution)/shard_map/all_to_all | solution.py:26
  35.9 19.2 %convert_bitcast_fusion = bf16[16,4,256,512]{2,3,1,0:T(8,128)(2,1)} fusion(bf16[16,4,256,512]{3,2,1,0:T(8,128)(2,1)} %bitcast.52, bf16[16,4,256,256]{3,2,1,0:T(8,128)(2,1)} %param.9), kind=kOutput, calls=%fused_computation.4 | convolution fusion | flops 4303355904 | bytes 41943040 | tf_op jit(solution)/shard_map/pqij,pqjd->pqid/dot_general | solution.py:18
  55.1 7.4 %all-to-all-start.2 = ((bf16[16,4,256,512]{2,3,1,0:T(8,128)(2,1)}), bf16[16,4,256,512]{2,3,1,0:T(8,128)(2,1)}, u32[]{:S(2)}, u32[]{:S(2)}) async-start(bf16[16,4,256,512]{2,3,1,0:T(8,128)(2,1)} %convert_bitcast_fusion), calls=%async_computation.2 | async-start | bytes 33554432 | tf_op jit(solution)/shard_map/all_to_all | solution.py:22
  62.6 14.5 %all_gather.3 = bf16[512,512]{1,0:T(8,128)(2,1)S(1)} all-gather(bf16[64,512]{1,0:T(8,128)(2,1)S(1)} %copy-done.6), channel_id=1, replica_groups=mesh['row'=8,'col'=16] {'row'}, dimensions={0}, use_global_device_ids=true | all-gather | bytes 589824 | tf_op jit(solution)/shard_map/all_gather | solution.py:48
  77.5 229.1 %all-to-all-done.2 = bf16[16,4,256,512]{2,3,1,0:T(8,128)(2,1)} async-done(((bf16[16,4,256,512]{2,3,1,0:T(8,128)(2,1)}), bf16[16,4,256,512]{2,3,1,0:T(8,128)(2,1)}, u32[]{:S(2)}, u32[]{:S(2)}) %all-to-all-start.2) | async-done | bytes 16777248 | tf_op jit(solution)/shard_map/all_to_all | solution.py:22
  306.6 24.3 %copy.33 = bf16[8,8,256,512]{3,1,2,0:T(8,128)(2,1)} copy(bf16[8,8,256,512]{2,3,1,0:T(8,128)(2,1)} %bitcast.36) | data formatting | bytes 33554432
  330.9 9.2 %divide_convert_fusion = bf16[16,256,512]{2,0,1:T(8,128)(2,1)S(1)} fusion(bf16[16,256,512]{2,1,0:T(8,128)(2,1)} %bitcast.54, f32[16]{0:T(128)S(1)} %broadcast_add_fusion, f32[64]{0:T(128)S(1)} %reshape.48, f32[64]{0:T(128)S(1)} %reshape.47, bf16[8,8,256,512]{3,1,2,0:T(8,128)(2,1)} %copy.33), kind=kOutput, calls=%fused_computation.10 | convolution fusion | flops 278923264 | bytes 25166400 | tf_op jit(solution)/shard_map/dot_general | solution.py:36
  340.1 2.4 copy.30
  342.5 5.7 multiply_convert_fusion.1
  348.2 10.1 %fusion.3 = bf16[512,4096]{0,1:T(8,128)(2,1)S(1)} fusion(bf16[4096,512]{1,0:T(8,128)(2,1)S(1)} %get-tuple-element.13, bf16[512,512]{1,0:T(8,128)(2,1)S(1)} %all_gather.3, s32[512]{0:T(512)S(1)} %bitcast.63, s32[512]{0:T(512)S(1)} %bitcast.64, s32[512]{0:T(512)S(1)} %bitcast.58, s32[512]{0:T(512)S(1)} %bitcast.59, s32[512]{0:T(512)S(1)} %bitcast.60, ...), kind=kOutput, calls=%fused_computation.6 | convolution fusion | flops 2195718144 | bytes 8945664 | tf_op jit(solution)/shard_map/nd,ld->nl/dot_general | solution.py:49
  358.3 1.9 copy-done.3
  360.2 3.3 fusion.15
  363.6 34.4 %reduce-scatter.2.cloned.1.call-done = f32[64,512]{1,0:T(8,128)} async-done(((f32[512,512]{1,0:T(8,128)}), f32[64,512]{1,0:T(8,128)}) %reduce-scatter.2.cloned.1.call-update) | async-done | bytes 131088 | tf_op jit(solution)/shard_map/reduce_scatter | solution.py:65
  399.4 12.6 %fusion.6 = f32[512,512]{1,0:T(8,128)} fusion(bf16[4096,512]{1,0:T(8,128)(2,1)} %bitcast.56, f32[4096,512]{1,0:T(8,128)} %get-tuple-element.12, bf16[512,4096]{0,1:T(8,128)(2,1)} %copy-done.3, bf16[512,512]{1,0:T(8,128)(2,1)S(1)} %all_gather.3), kind=kOutput, calls=%fused_computation.11 | convolution fusion | flops 4313841664 | bytes 18350080 | tf_op jit(solution)/shard_map/la,lb->ab/dot_general | solution.py:63
  412.1 2.9 collective-permute-start.1
  415.0 3.7 collective-permute-done.1
  418.7 1.5 collective-permute-start.2
  420.2 4.4 collective-permute-done.2
  424.6 3.1 collective-permute-start.3
  427.8 3.6 collective-permute-done.3
  432.1 126.7 %all-reduce.2.cloned.1.call-done = f32[512,512]{1,0:T(8,128)} async-done(((f32[512,512]{1,0:T(8,128)}), f32[512,512]{1,0:T(8,128)}) %all-reduce.2.cloned.1.call-update) | async-done | bytes 1048592 | tf_op jit(solution)/shard_map/psum | solution.py:64
  558.8 2.3 copy.43
  (43 shorter events, 6.3 us)
Async XLA Ops:
  8.0 334.5 %copy-start = (bf16[512,512]{1,0:T(8,128)(2,1)S(1)}, bf16[512,512]{1,0:T(8,128)(2,1)}, u32[]{:S(2)}) copy-start(bf16[512,512]{1,0:T(8,128)(2,1)} %param.13) | copy-start | bytes 1572868
  9.5 19.2 %all-to-all-start = ((bf16[16,1,4]{2,1,0:T(2,128)(2,1)}), bf16[16,1,4]{2,1,0:T(2,128)(2,1)S(1)}, u32[]{:S(2)}, u32[]{:S(2)}) async-start(bf16[16,1,4]{2,1,0:T(2,128)(2,1)} %copy.23), calls=%async_computation | async-start | bytes 16384 | tf_op jit(solution)/shard_map/all_to_all | solution.py:23
  28.7 26.4 %all-to-all-start.1 = ((bf16[16,1,4]{2,1,0:T(2,128)(2,1)}), bf16[16,1,4]{2,1,0:T(2,128)(2,1)S(1)}, u32[]{:S(2)}, u32[]{:S(2)}) async-start(bf16[16,1,4]{2,1,0:T(2,128)(2,1)} %copy.24), calls=%async_computation.1 | async-start | bytes 16384 | tf_op jit(solution)/shard_map/all_to_all | solution.py:26
  55.1 7.5 %copy-start.7 = (s32[512,8]{0,1:T(8,128)S(1)}, s32[512,8]{0,1:T(8,128)}, u32[]{:S(2)}) copy-start(s32[512,8]{0,1:T(8,128)} %param.15) | copy-start | bytes 49156
  55.1 7.5 %copy-start.6 = (bf16[64,512]{1,0:T(8,128)(2,1)S(1)}, bf16[64,512]{1,0:T(8,128)(2,1)}, u32[]{:S(2)}) copy-start(bf16[64,512]{1,0:T(8,128)(2,1)} %param.14) | copy-start | bytes 196612
  55.1 251.5 %all-to-all-start.2 = ((bf16[16,4,256,512]{2,3,1,0:T(8,128)(2,1)}), bf16[16,4,256,512]{2,3,1,0:T(8,128)(2,1)}, u32[]{:S(2)}, u32[]{:S(2)}) async-start(bf16[16,4,256,512]{2,3,1,0:T(8,128)(2,1)} %convert_bitcast_fusion), calls=%async_computation.2 | async-start | bytes 33554432 | tf_op jit(solution)/shard_map/all_to_all | solution.py:22
  62.5 335.5 %reduce-scatter.2.cloned.1.call-start = ((), (), s32[]{:S(2)}) async-start(), calls=%async_computation.4 | async-start | bytes 1179648 | tf_op jit(solution)/shard_map/reduce_scatter | solution.py:65
  342.5 5.7 copy-start.4
  348.2 10.1 %copy-start.2 = (bf16[4096,512]{1,0:T(8,128)(2,1)}, bf16[4096,512]{1,0:T(8,128)(2,1)S(1)}, u32[]{:S(2)}) copy-start(bf16[4096,512]{1,0:T(8,128)(2,1)S(1)} %get-tuple-element.13) | copy-start | bytes 12582916
  358.3 1.9 copy-start.3
  363.5 195.2 %all-reduce.2.cloned.1.call-start = ((), (), s32[]{:S(2)}) async-start(), calls=%async_computation.5 | async-start | bytes 2097152 | tf_op jit(solution)/shard_map/psum | solution.py:64
  398.0 14.0 %collective-permute-start = (f32[64,512]{1,0:T(8,128)}, f32[64,512]{1,0:T(8,128)S(1)}, u32[]{:S(2)}, u32[]{:S(2)}) collective-permute-start(f32[64,512]{1,0:T(8,128)} %reduce-scatter.2.cloned.1.call-done), channel_id=1, source_target_pairs={{0,1},{1,0},{2,3},{3,2},{4,5},{5,4},{6,7},{7,6},{8,9},{9,8},{10,11... | collective-permute-start | bytes 393224 | tf_op jit(solution)/shard_map/ppermute | solution.py:68
  399.4 12.7 %copy-start.5 = (f32[64,512]{1,0:T(8,128)S(1)}, f32[64,512]{1,0:T(8,128)}, u32[]{:S(2)}) copy-start(f32[64,512]{1,0:T(8,128)} %reduce-scatter.2.cloned.1.call-done) | copy-start | bytes 393220
  399.4 161.6 %copy-start.1 = (bf16[512,512]{1,0:T(8,128)(2,1)S(1)}, bf16[512,512]{1,0:T(8,128)(2,1)}, u32[]{:S(2)}) copy-start(bf16[512,512]{1,0:T(8,128)(2,1)} %param.13) | copy-start | bytes 1572868
  412.1 6.6 %collective-permute-start.1 = (f32[64,512]{1,0:T(8,128)S(1)}, f32[64,512]{1,0:T(8,128)S(1)}, u32[]{:S(2)}, u32[]{:S(2)}) collective-permute-start(f32[64,512]{1,0:T(8,128)S(1)} %add.67), channel_id=1, source_target_pairs={{0,2},{1,3},{2,0},{3,1},{4,6},{5,7},{6,4},{7,5},{8,10},{9,11},{10,... | collective-permute-start | bytes 393224 | tf_op jit(solution)/shard_map/ppermute | solution.py:68
  418.7 5.9 %collective-permute-start.2 = (f32[64,512]{1,0:T(8,128)S(1)}, f32[64,512]{1,0:T(8,128)S(1)}, u32[]{:S(2)}, u32[]{:S(2)}) collective-permute-start(f32[64,512]{1,0:T(8,128)S(1)} %add.68), channel_id=1, source_target_pairs={{0,4},{1,5},{2,6},{3,7},{4,0},{5,1},{6,2},{7,3},{8,12},{9,13},{10,... | collective-permute-start | bytes 393224 | tf_op jit(solution)/shard_map/ppermute | solution.py:68
  424.6 6.7 %collective-permute-start.3 = (f32[64,512]{1,0:T(8,128)S(1)}, f32[64,512]{1,0:T(8,128)S(1)}, u32[]{:S(2)}, u32[]{:S(2)}) collective-permute-start(f32[64,512]{1,0:T(8,128)S(1)} %add.69), channel_id=1, source_target_pairs={{0,8},{1,9},{2,10},{3,11},{4,12},{5,13},{6,14},{7,15},{8,0},{9,1},... | collective-permute-start | bytes 393224 | tf_op jit(solution)/shard_map/ppermute | solution.py:68
Sparse Core Ops, SparseCore 0:
  363.7 34.3 reduce-scatter.1
Sparse Core Ops, SparseCore 1:
  412.1 146.6 all-reduce.1
